TPU v7x, 256 devices: a whole 4x4x8 slice. The times are simulated.
256 devices in a mesh: blk: 64 (over y, x_hi, z), repl: 4 (over x_lo, core).
Axes of the slice: x: 4 (x_hi: 2, x_lo: 2; x = x_hi * 2 + x_lo), y: 4, z: 8, core: 2. Of those that a mesh axis runs over, the one named last changes fastest.
Arguments:
- feats: bfloat16 [131072, 512], P(('blk', 'repl')), may hold values from -6 to 6
- weight: bfloat16 [512, 512], replicated, may hold values from -0.25 to 0.25
- tile_vals: bfloat16 [1024, 8, 128, 128], P(('blk', 'repl')), may hold values from -0.25 to 0.25
- tile_cols: int32 [1024, 8], P(('blk', 'repl')), may hold values from 0 to 1023, as said below
- tile_count: int32 [1024], P(('blk', 'repl')), may hold values from 2 to 8, as said below
- cotangent: bfloat16 [131072, 512], P(('blk', 'repl')), may hold values from -24 to 24
Outputs:
- output: bfloat16 [131072, 512], P(('blk', 'repl'))
- weight_grad: float32 [512, 512], replicated
- feat_grad: bfloat16 [131072, 512], P(('blk', 'repl'))
Inputs may be any that keep to these rules, and one draw needn't show every extreme that they name: `tile_cols`: slot 0 of block row k names k itself. Every named column block lies in a panel (of 2048 nodes, block row k being in panel k * 128 // 2048) at most 2 panels away from its row's panel, counted around a closed cycle of panels. `tile_count`: slots at and after a block row's count are not part of the adjacency.
All inputs are finite; a program needn't handle non-finite values.
Results may differ from a plain program's by a relative error of at most 0.011.
Values may be sent and summed in bfloat16 or wider, within the bound.
A program may use at most 128 MiB of HBM per device.

v0:
```python
import math
import jax
import jax.numpy as jnp
from jax import lax
from jax.sharding import PartitionSpec as P

TILE = 128
SLOTS = 8
REACH = 2


def passed_along(value, axis, steps):
    count = lax.axis_size(axis)
    pairs = [(source, (source + steps) % count) for source in range(count)]
    return lax.ppermute(value, axis, pairs)


def shortened(x):
    return jax.tree.map(lambda a: a.astype(jnp.bfloat16) if a.dtype == jnp.float32 else a, x)


def from_everyone(x, axis):
    length = lax.axis_size(axis)
    return lax.all_to_all(jnp.broadcast_to(x[None], (length, *x.shape)), axis, 0, 0, tiled=True)


def laid_out(pieces, dim):
    lengths = list(pieces.shape[1:])
    lengths[dim] *= pieces.shape[0]
    return jnp.moveaxis(pieces, 0, dim).reshape(lengths)


def gathered_copies(x, axis, dim):
    pieces = from_everyone(x, axis)
    return laid_out(pieces, dim)


def silu_slope(preact):
    sigma = jax.nn.sigmoid(preact)
    return sigma * (1.0 + preact * (1.0 - sigma))


def window_index(tile_cols, center, panel_blocks, cycle_size):
    panel_of = tile_cols // panel_blocks
    offset = (panel_of - center) % cycle_size
    offset = jnp.where(offset > REACH, offset - cycle_size, offset)
    return (offset + REACH) * panel_blocks + tile_cols % panel_blocks


def shift_window(source):
    lower_side = []
    upper_side = []
    below_piece = source
    above_piece = source
    for hop_number in range(REACH):
        below_piece = passed_along(below_piece, "blk", 1)
        above_piece = passed_along(above_piece, "blk", -1)
        lower_side.append(below_piece)
        upper_side.append(above_piece)
    pieces = lower_side[::-1] + [source] + upper_side
    return pieces


def return_to_owners(shares):
    upward = jnp.zeros_like(shares[REACH])
    for offset in range(REACH, 0, -1):
        upward = passed_along(shortened(upward + shares[offset + REACH]), "blk", 1)
    downward = jnp.zeros_like(shares[REACH])
    for offset in range(-REACH, 0):
        downward = passed_along(shortened(downward + shares[offset + REACH]), "blk", -1)
    total = shares[REACH] + upward + downward
    return total


def local(feats, weight, tile_vals, tile_cols, tile_count, cotangent):
    node_rows = feats.shape[0]
    feat_width = feats.shape[1]
    cycle_size = lax.axis_size("blk")
    group_size = lax.axis_size("repl")
    panel_size = node_rows * group_size
    panel_blocks = panel_size // TILE
    block_rows = node_rows // TILE
    span_count = 2 * REACH + 1
    center = lax.axis_index("blk")
    own_panel = gathered_copies(feats, "repl", 0)
    pieces = shift_window(own_panel)
    window = jnp.concatenate(pieces, axis=0).reshape(span_count * panel_blocks, TILE, feat_width)
    local_index = window_index(tile_cols, center, panel_blocks, cycle_size)
    slot_ids = jnp.arange(SLOTS, dtype=jnp.int32)
    live_slots = slot_ids[None, :] < tile_count[:, None]
    masked_vals = jnp.where(live_slots[:, :, None, None], tile_vals, jnp.zeros_like(tile_vals))
    picked = window[local_index]
    summed = jnp.einsum("nsij,nsjf->nif", masked_vals, picked, preferred_element_type=jnp.float32)
    aggregate = summed.reshape(node_rows, feat_width).astype(jnp.bfloat16)
    preact = jnp.dot(aggregate, weight, preferred_element_type=jnp.float32)
    output = jax.nn.silu(preact).astype(jnp.bfloat16)
    slope = (cotangent.astype(jnp.float32) * silu_slope(preact)).astype(jnp.bfloat16)
    nodes_total = node_rows * group_size * cycle_size
    weight_term = jnp.einsum("nf,ng->fg", aggregate, slope, preferred_element_type=jnp.float32)
    weight_grad = lax.psum(weight_term, ("blk", "repl")) * (1.0 / math.sqrt(nodes_total))
    backward = jnp.einsum("nf,gf->ng", slope, weight, preferred_element_type=jnp.float32).astype(
        jnp.bfloat16
    )
    back_blocks = backward.reshape(block_rows, TILE, feat_width)
    segments = span_count * panel_blocks
    contrib = jnp.einsum(
        "nsji,njf->nsif", masked_vals, back_blocks, preferred_element_type=jnp.float32
    )
    partial_sums = jax.ops.segment_sum(
        contrib.reshape(block_rows * SLOTS, TILE, feat_width),
        local_index.reshape(-1),
        num_segments=segments,
    )
    panel_parts = partial_sums.reshape(span_count, panel_size, feat_width)
    shares = [panel_parts[position] for position in range(span_count)]
    panel_total = return_to_owners(shares)
    grad_rows = lax.psum_scatter(
        panel_total.astype(jnp.bfloat16), "repl", scatter_dimension=0, tiled=True
    )
    return (output, weight_grad, grad_rows)


def solution(mesh):
    in_specs = (
        P(("blk", "repl"), None),
        P(),
        P(("blk", "repl"), None, None, None),
        P(("blk", "repl"), None),
        P(("blk", "repl")),
        P(("blk", "repl"), None),
    )
    out_specs = (P(("blk", "repl"), None), P(), P(("blk", "repl"), None))
    return jax.shard_map(local, mesh=mesh, in_specs=in_specs, out_specs=out_specs, check_vma=False)
```

profile of v0, /device:TPU:2, one launch (start us, length us, event | category | flops | bytes accessed | tf_op | source)
XLA Modules:
  0.0 551.7 jit_solution(13088517721672567636)
XLA Ops:
  9.3 28.7 %all_to_all.5 = bf16[4,512,512]{2,1,0:T(8,128)(2,1)S(1)} all-to-all(bf16[4,512,512]{2,1,0:T(8,128)(2,1)S(1)} %broadcast_in_dim.28), channel_id=1, replica_groups=mesh['blk'=64,'repl'=4] {'repl'}, dimensions={0} | all-to-all | bytes 4194304 | tf_op jit(solution)/shard_map/all_to_all | solution.py:24
  38.4 8.2 %collective-permute-start.2 = (bf16[2048,512]{1,0:T(8,128)(2,1)S(1)}, bf16[2048,512]{1,0:T(8,128)(2,1)}, u32[]{:S(2)}, u32[]{:S(2)}) collective-permute-start(bf16[2048,512]{1,0:T(8,128)(2,1)S(1)} %bitcast.42), channel_id=1, source_target_pairs={{0,252},{4,0},{8,4},{12,8},{16,12},{20,16},{24,20},{28,24},{32,28}... | collective-permute-start | bytes 6291464 | tf_op jit(solution)/shard_map/ppermute | solution.py:15
  46.5 45.8 %collective-permute-done = bf16[2048,512]{1,0:T(8,128)(2,1)} collective-permute-done((bf16[2048,512]{1,0:T(8,128)(2,1)S(1)}, bf16[2048,512]{1,0:T(8,128)(2,1)}, u32[]{:S(2)}, u32[]{:S(2)}) %collective-permute-start) | collective-permute-done | bytes 2097184 | tf_op jit(solution)/shard_map/ppermute | solution.py:15
  92.3 7.7 %collective-permute-start.3 = (bf16[2048,512]{1,0:T(8,128)(2,1)}, bf16[2048,512]{1,0:T(8,128)(2,1)}, u32[]{:S(2)}, u32[]{:S(2)}) collective-permute-start(bf16[2048,512]{1,0:T(8,128)(2,1)} %collective-permute-done.2), channel_id=1, source_target_pairs={{0,252},{4,0},{8,4},{12,8},{16,12},{20,16},{24,20},{28,24},{32,28}... | collective-permute-start | bytes 6291464 | tf_op jit(solution)/shard_map/ppermute | solution.py:15
  100.4 44.9 %collective-permute-done.1 = bf16[2048,512]{1,0:T(8,128)(2,1)} collective-permute-done((bf16[2048,512]{1,0:T(8,128)(2,1)}, bf16[2048,512]{1,0:T(8,128)(2,1)}, u32[]{:S(2)}, u32[]{:S(2)}) %collective-permute-start.1) | collective-permute-done | bytes 2097184 | tf_op jit(solution)/shard_map/ppermute | solution.py:15
  152.3 4.0 copy-done.3
  156.3 7.0 %gather_fusion = bf16[32,128,512]{2,1,0:T(8,128)(2,1)} fusion(bf16[80,128,512]{2,1,0:T(8,128)(2,1)} %bitcast.44, s32[1024]{0:T(1024)S(1)} %pad_clamp_fusion), kind=kCustom, calls=%fused_computation | custom fusion | bytes 8388736 | tf_op jit(solution)/shard_map/gather | solution.py:92
  163.3 3.0 fusion.4
  168.4 4.6 fusion.5
  173.0 9.7 %broadcast_in_dim.30 = f32[80,128,512]{2,1,0:T(8,128)} broadcast(f32[]{:T(128)} %constant.63.clone.1), dimensions={} | broadcast | bytes 20971524 | tf_op jit(solution)/shard_map/broadcast_in_dim | solution.py:109
  182.6 18.8 %scatter_fusion = f32[80,128,512]{2,1,0:T(8,128)} fusion(f32[80,128,512]{2,1,0:T(8,128)} %broadcast_in_dim.30, s32[32]{0:T(128)S(1)} %reshape.69, f32[32,128,512]{2,1,0:T(8,128)} %bitcast.39), kind=kCustom, calls=%fused_computation.1 | custom fusion | flops 2097152 | bytes 25165952 | tf_op jit(solution)/shard_map/scatter-add | solution.py:109
  201.5 8.0 %convert.4 = bf16[80,128,512]{2,1,0:T(8,128)(2,1)S(1)} convert(f32[80,128,512]{2,1,0:T(8,128)} %scatter_fusion) | non-fusion elementwise | flops 5242880 | bytes 31457280 | tf_op jit(solution)/shard_map/convert.1
  209.4 2.3 fusion.18
  211.7 1.8 collective-permute-start.6
  213.7 10.1 %fusion.17 = (f32[16,128,512]{2,1,0:T(8,128)S(1)}, f32[16,128,512]{2,1,0:T(8,128)}, f32[16,128,512]{2,1,0:T(8,128)}) fusion(f32[80,128,512]{2,1,0:T(8,128)} %scatter_fusion), kind=kLoop, calls=%fused_computation.46 | loop fusion | bytes 25165824 | tf_op jit(solution)/shard_map/slice | solution.py:115
  223.9 33.9 %collective-permute-done.6 = bf16[2048,512]{1,0:T(8,128)(2,1)} collective-permute-done((bf16[2048,512]{1,0:T(8,128)(2,1)}, bf16[2048,512]{1,0:T(8,128)(2,1)}, u32[]{:S(2)}, u32[]{:S(2)}) %collective-permute-start.6) | collective-permute-done | bytes 2097184 | tf_op jit(solution)/shard_map/ppermute | solution.py:15
  257.8 4.9 fusion
  262.7 7.7 %collective-permute-start.7 = (bf16[2048,512]{1,0:T(8,128)(2,1)}, bf16[2048,512]{1,0:T(8,128)(2,1)}, u32[]{:S(2)}, u32[]{:S(2)}) collective-permute-start(bf16[2048,512]{1,0:T(8,128)(2,1)} %fusion), channel_id=1, source_target_pairs={{0,252},{4,0},{8,4},{12,8},{16,12},{20,16},{24,20},{28,24},{32,28}... | collective-permute-start | bytes 6291464 | tf_op jit(solution)/shard_map/ppermute | solution.py:15
  270.4 4.1 fusion.1
  276.0 38.6 %collective-permute-done.7 = bf16[2048,512]{1,0:T(8,128)(2,1)} collective-permute-done((bf16[2048,512]{1,0:T(8,128)(2,1)}, bf16[2048,512]{1,0:T(8,128)(2,1)}, u32[]{:S(2)}, u32[]{:S(2)}) %collective-permute-start.7) | collective-permute-done | bytes 2097184 | tf_op jit(solution)/shard_map/ppermute | solution.py:15
  314.6 12.3 %collective-permute-done.5 = bf16[2048,512]{1,0:T(8,128)(2,1)S(1)} collective-permute-done((bf16[2048,512]{1,0:T(8,128)(2,1)}, bf16[2048,512]{1,0:T(8,128)(2,1)S(1)}, u32[]{:S(2)}, u32[]{:S(2)}) %collective-permute-start.5) | collective-permute-done | bytes 2097184 | tf_op jit(solution)/shard_map/ppermute | solution.py:15
  327.0 5.1 fusion.3
  332.1 209.8 %all-reduce.2.cloned.1.call-done = f32[512,512]{1,0:T(8,128)} async-done(((f32[512,512]{1,0:T(8,128)}), f32[512,512]{1,0:T(8,128)}) %all-reduce.2.cloned.1.call-update) | async-done | bytes 1048592 | tf_op jit(solution)/shard_map/psum | solution.py:100
  541.9 2.3 broadcast_multiply_fusion
  (43 shorter events, 12.7 us)
Async XLA Ops:
  8.0 158.3 %copy-start = (bf16[512,512]{1,0:T(8,128)(2,1)S(1)}, bf16[512,512]{1,0:T(8,128)(2,1)}, u32[]{:S(2)}) copy-start(bf16[512,512]{1,0:T(8,128)(2,1)} %param.7) | copy-start | bytes 1572868
  8.0 92.1 %copy-start.6 = (s32[4,8]{1,0:T(4,128)S(1)}, s32[4,8]{1,0:T(4,128)}, u32[]{:S(2)}) copy-start(s32[4,8]{1,0:T(4,128)} %param.9) | copy-start | bytes 388
  8.0 92.3 %copy-start.8 = (s32[4]{0:T(128)S(1)}, s32[4]{0:T(128)}, u32[]{:S(2)}) copy-start(s32[4]{0:T(128)} %param.10) | copy-start | bytes 52
  8.0 533.9 %all-reduce.2.cloned.1.call-start = ((), (), s32[]{:S(2)}) async-start(), calls=%async_computation.2 | async-start | bytes 2097152 | tf_op jit(solution)/shard_map/psum | solution.py:100
  38.1 54.2 %collective-permute-start = (bf16[2048,512]{1,0:T(8,128)(2,1)S(1)}, bf16[2048,512]{1,0:T(8,128)(2,1)}, u32[]{:S(2)}, u32[]{:S(2)}) collective-permute-start(bf16[2048,512]{1,0:T(8,128)(2,1)S(1)} %bitcast.41), channel_id=1, source_target_pairs={{0,4},{4,8},{8,12},{12,16},{16,20},{20,24},{24,28},{28,32},{32,36}... | collective-permute-start | bytes 6291464 | tf_op jit(solution)/shard_map/ppermute | solution.py:15
  38.4 53.9 %collective-permute-start.2 = (bf16[2048,512]{1,0:T(8,128)(2,1)S(1)}, bf16[2048,512]{1,0:T(8,128)(2,1)}, u32[]{:S(2)}, u32[]{:S(2)}) collective-permute-start(bf16[2048,512]{1,0:T(8,128)(2,1)S(1)} %bitcast.42), channel_id=1, source_target_pairs={{0,252},{4,0},{8,4},{12,8},{16,12},{20,16},{24,20},{28,24},{32,28}... | collective-permute-start | bytes 6291464 | tf_op jit(solution)/shard_map/ppermute | solution.py:15
  92.3 52.9 %collective-permute-start.1 = (bf16[2048,512]{1,0:T(8,128)(2,1)}, bf16[2048,512]{1,0:T(8,128)(2,1)}, u32[]{:S(2)}, u32[]{:S(2)}) collective-permute-start(bf16[2048,512]{1,0:T(8,128)(2,1)} %collective-permute-done), channel_id=1, source_target_pairs={{0,4},{4,8},{8,12},{12,16},{16,20},{20,24},{24,28},{28,32},{32,36}... | collective-permute-start | bytes 6291464 | tf_op jit(solution)/shard_map/ppermute | solution.py:15
  92.3 58.2 %collective-permute-start.3 = (bf16[2048,512]{1,0:T(8,128)(2,1)}, bf16[2048,512]{1,0:T(8,128)(2,1)}, u32[]{:S(2)}, u32[]{:S(2)}) collective-permute-start(bf16[2048,512]{1,0:T(8,128)(2,1)} %collective-permute-done.2), channel_id=1, source_target_pairs={{0,252},{4,0},{8,4},{12,8},{16,12},{20,16},{24,20},{28,24},{32,28}... | collective-permute-start | bytes 6291464 | tf_op jit(solution)/shard_map/ppermute | solution.py:15
  152.3 4.0 copy-start.3
  156.3 7.0 %copy-start.2 = (bf16[4,8,128,128]{3,2,1,0:T(8,128)(2,1)S(1)}, bf16[4,8,128,128]{3,2,1,0:T(8,128)(2,1)}, u32[]{:S(2)}) copy-start(bf16[4,8,128,128]{3,2,1,0:T(8,128)(2,1)} %param.8) | copy-start | bytes 3145732
  163.3 3.0 copy-start.7
  166.3 2.1 copy-start.4
  211.7 46.1 %collective-permute-start.6 = (bf16[2048,512]{1,0:T(8,128)(2,1)}, bf16[2048,512]{1,0:T(8,128)(2,1)}, u32[]{:S(2)}, u32[]{:S(2)}) collective-permute-start(bf16[2048,512]{1,0:T(8,128)(2,1)} %bitcast.13), channel_id=1, source_target_pairs={{0,252},{4,0},{8,4},{12,8},{16,12},{20,16},{24,20},{28,24},{32,28}... | collective-permute-start | bytes 6291464 | tf_op jit(solution)/shard_map/ppermute | solution.py:15
  213.5 56.9 %collective-permute-start.4 = (bf16[2048,512]{1,0:T(8,128)(2,1)}, bf16[2048,512]{1,0:T(8,128)(2,1)}, u32[]{:S(2)}, u32[]{:S(2)}) collective-permute-start(bf16[2048,512]{1,0:T(8,128)(2,1)} %bitcast.11), channel_id=1, source_target_pairs={{0,4},{4,8},{8,12},{12,16},{16,20},{20,24},{24,28},{28,32},{32,36}... | collective-permute-start | bytes 6291464 | tf_op jit(solution)/shard_map/ppermute | solution.py:15
  262.7 51.9 %collective-permute-start.7 = (bf16[2048,512]{1,0:T(8,128)(2,1)}, bf16[2048,512]{1,0:T(8,128)(2,1)}, u32[]{:S(2)}, u32[]{:S(2)}) collective-permute-start(bf16[2048,512]{1,0:T(8,128)(2,1)} %fusion), channel_id=1, source_target_pairs={{0,252},{4,0},{8,4},{12,8},{16,12},{20,16},{24,20},{28,24},{32,28}... | collective-permute-start | bytes 6291464 | tf_op jit(solution)/shard_map/ppermute | solution.py:15
  270.4 4.1 copy-start.5
  274.5 52.5 %collective-permute-start.5 = (bf16[2048,512]{1,0:T(8,128)(2,1)}, bf16[2048,512]{1,0:T(8,128)(2,1)S(1)}, u32[]{:S(2)}, u32[]{:S(2)}) collective-permute-start(bf16[2048,512]{1,0:T(8,128)(2,1)} %fusion.1), channel_id=1, source_target_pairs={{0,4},{4,8},{8,12},{12,16},{16,20},{20,24},{24,28},{28,32},{32,36}... | collective-permute-start | bytes 6291464 | tf_op jit(solution)/shard_map/ppermute | solution.py:15
  275.9 268.3 %reduce-scatter.2.cloned.1.call-start = ((), (), s32[]{:S(2)}) async-start(), calls=%async_computation.3 | async-start | bytes 2621440 | tf_op jit(solution)/shard_map/reduce_scatter | solution.py:117
  327.0 217.3 %copy-start.1 = (bf16[512,512]{1,0:T(8,128)(2,1)S(1)}, bf16[512,512]{1,0:T(8,128)(2,1)}, u32[]{:S(2)}) copy-start(bf16[512,512]{1,0:T(8,128)(2,1)} %param.7) | copy-start | bytes 1572868
Sparse Core Ops, SparseCore 0:
  276.1 265.8 all-reduce.1
Sparse Core Ops, SparseCore 1:
  332.2 21.3 reduce-scatter.1
where the time goes:
time: 552 us
  waiting for transfers between devices  385 us (70%)
  other arithmetic  43.4 us (8%)
  local copies, waits for them, and re-layouts  41.5 us (8%)
  blocking collectives  28.7 us (5%)
  starting transfers between devices  26 us (5%)
  between operations  15.6 us (3%)
  matrix products  11.1 us (2%)
    psum x1, waiting for transfers between devices, local(): lax.psum(weight_term, ('blk', 'repl')) * (1.0 / math.sqrt(nodes_total))  210 us
    ppermute x8, waiting for transfers between devices, passed_along(): return lax.ppermute(value, axis, pairs)  176 us
    all_to_all x1, blocking collectives, from_everyone(): lax.all_to_all(jnp.broadcast_to(x[None], (length, *x.shape)), axis, 0, 0,...  28.7 us
    ppermute x8, starting transfers between devices, passed_along(): return lax.ppermute(value, axis, pairs)  25.9 us
    scatter-add x1, other arithmetic, local(): jax.ops.segment_sum(contrib.reshape(block_rows * SLOTS, TILE, feat_width)...  18.8 us
    slice x2, local copies, waits for them, and re-layouts, local(): shares = [panel_parts[position] for position in range(span_count)]  12.4 us
  transfers between devices with their start and end apart: 10, of which 6 were waited for; matrix products, arithmetic and copies ran while one was open for 6% of the time, Pallas kernels for 0%

commit v1 on v0

--- a/solution.py
+++ b/solution.py
@@ -97,7 +97,7 @@
     slope = (cotangent.astype(jnp.float32) * silu_slope(preact)).astype(jnp.bfloat16)
     nodes_total = node_rows * group_size * cycle_size
     weight_term = jnp.einsum("nf,ng->fg", aggregate, slope, preferred_element_type=jnp.float32)
-    weight_grad = lax.psum(weight_term, ("blk", "repl")) * (1.0 / math.sqrt(nodes_total))
+    weight_grad = lax.psum(lax.psum(weight_term, "repl"), "blk") * (1.0 / math.sqrt(nodes_total))
     backward = jnp.einsum("nf,gf->ng", slope, weight, preferred_element_type=jnp.float32).astype(
         jnp.bfloat16
     )

time: 552 us -> 1090 us (1.97)
  waiting for transfers between devices: 385 us -> 924 us
    psum x1 -> x2, waiting for transfers between devices: 210 us -> 772 us  [the longest x1 698 us: local(): lax.psum(lax.psum(weight_term, 'repl'), 'blk')]
    ppermute x8, waiting for transfers between devices: 176 us -> 125 us  [passed_along(): return lax.ppermute(value, axis, pairs)]
    reduce_scatter x1, waiting for transfers between devices: 0.01 us -> 28 us  [local(): lax.psum_scatter(panel_total.astype(jnp.bfloat16), 'repl', scatter_dimens...]
  transfers between devices with their start and end apart: 10 -> 11, of which waited for: 6 -> 6; matrix products, arithmetic and copies ran while one was open for 6% -> 3% of each run, Pallas kernels for 0% -> 0%
where the time goes in v1:
time: 1090 us
  waiting for transfers between devices  924 us (85%)
  other arithmetic  43.3 us (4%)
  local copies, waits for them, and re-layouts  41.5 us (4%)
  blocking collectives  28.7 us (3%)
  starting transfers between devices  26 us (2%)
  between operations  13.9 us (1%)
  matrix products  11.1 us (1%)
    psum x1, waiting for transfers between devices, local(): lax.psum(lax.psum(weight_term, 'repl'), 'blk')  698 us
    ppermute x8, waiting for transfers between devices, passed_along(): return lax.ppermute(value, axis, pairs)  125 us
    psum x1, waiting for transfers between devices, local(): lax.psum(weight_term, 'repl')  74.2 us
    all_to_all x1, blocking collectives, from_everyone(): lax.all_to_all(jnp.broadcast_to(x[None], (length, *x.shape)), axis, 0, 0,...  28.7 us
    reduce_scatter x1, waiting for transfers between devices, local(): lax.psum_scatter(panel_total.astype(jnp.bfloat16), 'repl', scatter_dimens...  28 us
    ppermute x8, starting transfers between devices, passed_along(): return lax.ppermute(value, axis, pairs)  25.9 us
  transfers between devices with their start and end apart: 11, of which 6 were waited for; matrix products, arithmetic and copies ran while one was open for 3% of the time, Pallas kernels for 0%

profile of v1, /device:TPU:2, one launch (start us, length us, event | category | flops | bytes accessed | tf_op | source)
XLA Modules:
  0.0 1088.9 jit_solution(8382876286018407745)
XLA Ops:
  8.5 28.7 %all_to_all.5 = bf16[4,512,512]{2,1,0:T(8,128)(2,1)S(1)} all-to-all(bf16[4,512,512]{2,1,0:T(8,128)(2,1)S(1)} %broadcast_in_dim.28), channel_id=1, replica_groups=mesh['blk'=64,'repl'=4] {'repl'}, dimensions={0} | all-to-all | bytes 4194304 | tf_op jit(solution)/shard_map/all_to_all | solution.py:24
  37.6 8.2 collective-permute-start.2
  45.7 45.8 %collective-permute-done = bf16[2048,512]{1,0:T(8,128)(2,1)} collective-permute-done((bf16[2048,512]{1,0:T(8,128)(2,1)S(1)}, bf16[2048,512]{1,0:T(8,128)(2,1)}, u32[]{:S(2)}, u32[]{:S(2)}) %collective-permute-start) | collective-permute-done | bytes 2097184 | tf_op jit(solution)/shard_map/ppermute | solution.py:15
  91.5 7.7 collective-permute-start.3
  99.5 44.9 %collective-permute-done.1 = bf16[2048,512]{1,0:T(8,128)(2,1)} collective-permute-done((bf16[2048,512]{1,0:T(8,128)(2,1)}, bf16[2048,512]{1,0:T(8,128)(2,1)}, u32[]{:S(2)}, u32[]{:S(2)}) %collective-permute-start.1) | collective-permute-done | bytes 2097184 | tf_op jit(solution)/shard_map/ppermute | solution.py:15
  151.5 4.0 copy-done.3
  155.5 7.0 gather_fusion
  162.4 3.0 fusion.4
  167.5 4.6 fusion.5
  172.2 9.7 broadcast_in_dim.30
  181.8 18.8 %scatter_fusion = f32[80,128,512]{2,1,0:T(8,128)} fusion(f32[80,128,512]{2,1,0:T(8,128)} %broadcast_in_dim.30, s32[32]{0:T(128)S(1)} %reshape.69, f32[32,128,512]{2,1,0:T(8,128)} %bitcast.39), kind=kCustom, calls=%fused_computation.1 | custom fusion | flops 2097152 | bytes 25165952 | tf_op jit(solution)/shard_map/scatter-add | solution.py:109
  200.6 8.0 convert.4
  208.6 2.3 fusion.18
  210.9 1.8 collective-permute-start.6
  212.9 10.1 fusion.17
  223.0 33.9 %collective-permute-done.6 = bf16[2048,512]{1,0:T(8,128)(2,1)} collective-permute-done((bf16[2048,512]{1,0:T(8,128)(2,1)}, bf16[2048,512]{1,0:T(8,128)(2,1)}, u32[]{:S(2)}, u32[]{:S(2)}) %collective-permute-start.6) | collective-permute-done | bytes 2097184 | tf_op jit(solution)/shard_map/ppermute | solution.py:15
  257.0 4.9 fusion
  261.9 7.6 collective-permute-start.7
  269.6 4.1 fusion.1
  275.1 74.2 %all-reduce.3.cloned.1.call-done = f32[512,512]{1,0:T(8,128)} async-done(((f32[512,512]{1,0:T(8,128)}), f32[512,512]{1,0:T(8,128)}) %all-reduce.3.cloned.1.call-update) | async-done | bytes 1048592 | tf_op jit(solution)/shard_map/psum | solution.py:100
  349.4 5.1 fusion.3
  354.6 697.5 %all-reduce.5.cloned.1.call-done = f32[512,512]{1,0:T(8,128)} async-done(((f32[512,512]{1,0:T(8,128)}), f32[512,512]{1,0:T(8,128)}) %all-reduce.5.cloned.1.call-update) | async-done | bytes 1048592 | tf_op jit(solution)/shard_map/psum | solution.py:100
  1052.1 2.3 broadcast_multiply_fusion
  1054.4 28.0 %reduce-scatter.2.cloned.1.call-done = bf16[512,512]{1,0:T(8,128)(2,1)} async-done(((bf16[2048,512]{1,0:T(8,128)(2,1)}), bf16[512,512]{1,0:T(8,128)(2,1)}) %reduce-scatter.2.cloned.1.call-update) | async-done | bytes 524304 | tf_op jit(solution)/shard_map/reduce_scatter | solution.py:117
  (46 shorter events, 12.8 us)
Async XLA Ops:
  7.2 158.3 %copy-start = (bf16[512,512]{1,0:T(8,128)(2,1)S(1)}, bf16[512,512]{1,0:T(8,128)(2,1)}, u32[]{:S(2)}) copy-start(bf16[512,512]{1,0:T(8,128)(2,1)} %param.7) | copy-start | bytes 1572868
  7.2 92.1 %copy-start.6 = (s32[4,8]{1,0:T(4,128)S(1)}, s32[4,8]{1,0:T(4,128)}, u32[]{:S(2)}) copy-start(s32[4,8]{1,0:T(4,128)} %param.9) | copy-start | bytes 388
  7.2 92.3 %copy-start.8 = (s32[4]{0:T(128)S(1)}, s32[4]{0:T(128)}, u32[]{:S(2)}) copy-start(s32[4]{0:T(128)} %param.10) | copy-start | bytes 52
  7.2 342.1 %all-reduce.3.cloned.1.call-start = ((), (), s32[]{:S(2)}) async-start(), calls=%async_computation.2 | async-start | bytes 2097152 | tf_op jit(solution)/shard_map/psum | solution.py:100
  37.2 54.2 %collective-permute-start = (bf16[2048,512]{1,0:T(8,128)(2,1)S(1)}, bf16[2048,512]{1,0:T(8,128)(2,1)}, u32[]{:S(2)}, u32[]{:S(2)}) collective-permute-start(bf16[2048,512]{1,0:T(8,128)(2,1)S(1)} %bitcast.41), channel_id=1, source_target_pairs={{0,4},{4,8},{8,12},{12,16},{16,20},{20,24},{24,28},{28,32},{32,36}... | collective-permute-start | bytes 6291464 | tf_op jit(solution)/shard_map/ppermute | solution.py:15
  37.6 53.9 %collective-permute-start.2 = (bf16[2048,512]{1,0:T(8,128)(2,1)S(1)}, bf16[2048,512]{1,0:T(8,128)(2,1)}, u32[]{:S(2)}, u32[]{:S(2)}) collective-permute-start(bf16[2048,512]{1,0:T(8,128)(2,1)S(1)} %bitcast.42), channel_id=1, source_target_pairs={{0,252},{4,0},{8,4},{12,8},{16,12},{20,16},{24,20},{28,24},{32,28}... | collective-permute-start | bytes 6291464 | tf_op jit(solution)/shard_map/ppermute | solution.py:15
  91.5 52.9 %collective-permute-start.1 = (bf16[2048,512]{1,0:T(8,128)(2,1)}, bf16[2048,512]{1,0:T(8,128)(2,1)}, u32[]{:S(2)}, u32[]{:S(2)}) collective-permute-start(bf16[2048,512]{1,0:T(8,128)(2,1)} %collective-permute-done), channel_id=1, source_target_pairs={{0,4},{4,8},{8,12},{12,16},{16,20},{20,24},{24,28},{28,32},{32,36}... | collective-permute-start | bytes 6291464 | tf_op jit(solution)/shard_map/ppermute | solution.py:15
  91.5 58.2 %collective-permute-start.3 = (bf16[2048,512]{1,0:T(8,128)(2,1)}, bf16[2048,512]{1,0:T(8,128)(2,1)}, u32[]{:S(2)}, u32[]{:S(2)}) collective-permute-start(bf16[2048,512]{1,0:T(8,128)(2,1)} %collective-permute-done.2), channel_id=1, source_target_pairs={{0,252},{4,0},{8,4},{12,8},{16,12},{20,16},{24,20},{28,24},{32,28}... | collective-permute-start | bytes 6291464 | tf_op jit(solution)/shard_map/ppermute | solution.py:15
  151.5 4.0 copy-start.3
  155.5 7.0 copy-start.2
  162.4 3.0 copy-start.7
  165.4 2.1 copy-start.4
  210.9 46.1 %collective-permute-start.6 = (bf16[2048,512]{1,0:T(8,128)(2,1)}, bf16[2048,512]{1,0:T(8,128)(2,1)}, u32[]{:S(2)}, u32[]{:S(2)}) collective-permute-start(bf16[2048,512]{1,0:T(8,128)(2,1)} %bitcast.13), channel_id=1, source_target_pairs={{0,252},{4,0},{8,4},{12,8},{16,12},{20,16},{24,20},{28,24},{32,28}... | collective-permute-start | bytes 6291464 | tf_op jit(solution)/shard_map/ppermute | solution.py:15
  212.7 56.9 %collective-permute-start.4 = (bf16[2048,512]{1,0:T(8,128)(2,1)}, bf16[2048,512]{1,0:T(8,128)(2,1)}, u32[]{:S(2)}, u32[]{:S(2)}) collective-permute-start(bf16[2048,512]{1,0:T(8,128)(2,1)} %bitcast.11), channel_id=1, source_target_pairs={{0,4},{4,8},{8,12},{12,16},{16,20},{20,24},{24,28},{28,32},{32,36}... | collective-permute-start | bytes 6291464 | tf_op jit(solution)/shard_map/ppermute | solution.py:15
  261.9 87.5 %collective-permute-start.7 = (bf16[2048,512]{1,0:T(8,128)(2,1)}, bf16[2048,512]{1,0:T(8,128)(2,1)}, u32[]{:S(2)}, u32[]{:S(2)}) collective-permute-start(bf16[2048,512]{1,0:T(8,128)(2,1)} %fusion), channel_id=1, source_target_pairs={{0,252},{4,0},{8,4},{12,8},{16,12},{20,16},{24,20},{28,24},{32,28}... | collective-permute-start | bytes 6291464 | tf_op jit(solution)/shard_map/ppermute | solution.py:15
  269.6 4.1 copy-start.5
  273.6 75.7 %collective-permute-start.5 = (bf16[2048,512]{1,0:T(8,128)(2,1)}, bf16[2048,512]{1,0:T(8,128)(2,1)S(1)}, u32[]{:S(2)}, u32[]{:S(2)}) collective-permute-start(bf16[2048,512]{1,0:T(8,128)(2,1)} %fusion.1), channel_id=1, source_target_pairs={{0,4},{4,8},{8,12},{12,16},{16,20},{20,24},{24,28},{28,32},{32,36}... | collective-permute-start | bytes 6291464 | tf_op jit(solution)/shard_map/ppermute | solution.py:15
  275.1 777.0 %all-reduce.5.cloned.1.call-start = ((), (), s32[]{:S(2)}) async-start(), calls=%async_computation.3 | async-start | bytes 2097152 | tf_op jit(solution)/shard_map/psum | solution.py:100
  349.3 733.0 %reduce-scatter.2.cloned.1.call-start = ((), (), s32[]{:S(2)}) async-start(), calls=%async_computation.4 | async-start | bytes 2621440 | tf_op jit(solution)/shard_map/reduce_scatter | solution.py:117
  349.4 733.0 %copy-start.1 = (bf16[512,512]{1,0:T(8,128)(2,1)S(1)}, bf16[512,512]{1,0:T(8,128)(2,1)}, u32[]{:S(2)}) copy-start(bf16[512,512]{1,0:T(8,128)(2,1)} %param.7) | copy-start | bytes 1572868
Sparse Core Ops, SparseCore 0:
  275.2 74.0 all-reduce.2
  351.9 700.1 all-reduce.4
  1055.2 27.1 reduce-scatter.1
